TPU v7x, 32 devices: a whole 2x2x4 slice. The times are simulated.
32 devices in a mesh: member: 4 (over x, core), tile: 4 (over z), grp: 2 (over y).
Axes of the slice: x: 2, y: 2, z: 4, core: 2. Of those that a mesh axis runs over, the one named last changes fastest.
Arguments:
- members: float32 [80, 128, 1024], P(('member', 'grp'), 'tile'), may hold values from -6 to 6
- courant_x: float32 [128, 1024], P('tile'), may hold values from -0.48 to 0.48
- courant_y: float32 [128, 1024], P('tile'), may hold values from -0.48 to 0.48
- obs_cell: int32 [4, 8, 1024], P('tile', ('member', 'grp')), may hold values from 0 to 4095
- innovation: float32 [4, 8, 1024], P('tile', ('member', 'grp')), may hold values from -6 to 6
- obs_weight: float32 [4, 8, 1024], P('tile', ('member', 'grp')), may hold values from 0.5 to 3
- stencil_offsets: int32 [9, 2], replicated, may hold values from -2 to 2, as said below
- stencil_weights: float32 [9], replicated, may hold values from 0.2 to 1
Outputs:
- analysis: float32 [80, 128, 1024], P(('member', 'grp'), 'tile')
- increment: float32 [128, 1024], P('tile', ('member', 'grp'))
Inputs may be any that keep to these rules, and one draw needn't show every extreme that they name: `stencil_offsets`: each row is a stencil entry's offsets along rows and columns; some entry reaches 2 cells along rows and some along columns. `obs_cell`: cells of a block are numbered row by row, 128 to a row.
All inputs are finite; a program needn't handle non-finite values.
Results may differ from a plain program's by a relative error of at most 0.0001.
Values sent between devices are 32-bit elements; how exact they have to be, the bound alone decides.
A program may use at most 128 MiB of HBM per device.

v0:
```python
import math
import jax
import jax.numpy as jnp
from jax import lax
from jax.sharding import PartitionSpec as P

RADIUS = 2
FSTEPS = 3
STEP_SIZE = 0.25
GROUP = ("member", "grp")


def halo(cells, axis, width, dim):
    count = lax.axis_size(axis)
    head = lax.slice_in_dim(cells, 0, width, axis=dim)
    tail = lax.slice_in_dim(cells, cells.shape[dim] - width, cells.shape[dim], axis=dim)
    above = lax.ppermute(tail, axis, [(i, i + 1) for i in range(count - 1)])
    below = lax.ppermute(head, axis, [(i + 1, i) for i in range(count - 1)])
    return jnp.concatenate([above, cells, below], axis=dim)


def upwind(q, cx, cy):
    rows = q.shape[1]
    c = q[:, 1:-1]
    left = jnp.pad(c, ((0, 0), (0, 0), (1, 0)))[:, :, :-1]
    right = jnp.pad(c, ((0, 0), (0, 0), (0, 1)))[:, :, 1:]
    return (
        c
        - jnp.maximum(cx, 0.0) * (c - q[:, : rows - 2])
        - jnp.minimum(cx, 0.0) * (q[:, 2:] - c)
        - jnp.maximum(cy, 0.0) * (c - left)
        - jnp.minimum(cy, 0.0) * (right - c)
    )


def spread_out(f, taps, sign):
    rows = f.shape[1] - 2 * RADIUS
    cols = f.shape[2]
    g = jnp.pad(f, ((0, 0), (0, 0), (RADIUS, RADIUS)))
    total = 0.0
    for r in range(-RADIUS, RADIUS + 1):
        for c in range(-RADIUS, RADIUS + 1):
            part = g[
                :,
                RADIUS + sign * r : RADIUS + sign * r + rows,
                RADIUS + sign * c : RADIUS + sign * c + cols,
            ]
            total = total + taps[r + RADIUS, c + RADIUS] * part
    return total


def on_device(members, courant_x, courant_y, obs_cell, innovation, obs_weight, offsets, weights):
    n, rows, cols = members.shape
    reach = 2 * RADIUS
    edge = reach + FSTEPS
    groups = lax.axis_size(GROUP)
    total = n * groups
    tile = lax.axis_index("tile")
    tiles = lax.axis_size("tile")
    packed = halo(jnp.concatenate([members, courant_x[None], courant_y[None]]), "tile", edge, 1)
    q, cx, cy = (packed[:n], packed[n], packed[n + 1])
    for s in range(FSTEPS):
        lo, hi = (s + 1, rows + 2 * edge - s - 1)
        q = upwind(q, cx[lo:hi], cy[lo:hi])
    fields = q[:, reach : reach + rows]
    own = jnp.sum(q, axis=0) / n
    mean = lax.psum(own, GROUP) / groups
    dev = (q - own[None]) / math.sqrt(total - 1)
    shift = (own - mean) * math.sqrt(n / (total - 1))
    ones = jnp.full_like(own, 1.0 / math.sqrt(groups))
    dev = jnp.concatenate([dev, shift[None], ones[None]])
    kr = jnp.arange(-RADIUS, RADIUS + 1)
    hit = (offsets[:, 0][:, None, None] == kr[None, :, None]) & (
        offsets[:, 1][:, None, None] == kr[None, None, :]
    )
    taps = jnp.sum(jnp.where(hit, weights[:, None, None], 0.0), axis=0) / jnp.sum(weights)
    at = jnp.arange(rows + 2 * RADIUS) - RADIUS + tile * rows
    inside = ((at >= 0) & (at < tiles * rows)).astype(jnp.float32)[None, :, None]

    def apply(h):
        z = spread_out(dev * h[None], taps, -1) * inside
        y = spread_out(z, taps, 1)
        return jnp.sum(dev[:, reach : reach + rows] * y, axis=0) * -STEP_SIZE

    width = cols // groups
    cell = obs_cell.reshape(-1)
    w = obs_weight.reshape(-1)
    wi = w * innovation.reshape(-1)
    pick_r = (cell[None] // width == jnp.arange(rows)[:, None]).astype(jnp.float32)
    pick_c = (cell[:, None] % width == jnp.arange(width)[None]).astype(jnp.float32)
    both = jnp.dot(
        jnp.concatenate([pick_r * w[None], pick_r * wi[None]]),
        pick_c,
        precision=lax.Precision.HIGHEST,
    )
    dense_w, dense_wi = (both[:rows], both[rows:])

    def gathered(block):
        return halo(lax.all_gather(block, GROUP, axis=1, tiled=True), "tile", reach, 0)

    x0 = lax.psum_scatter(apply(gathered(-dense_wi)), GROUP, scatter_dimension=1, tiled=True)
    g1 = dense_w * x0 - dense_wi
    x1 = lax.psum_scatter(apply(gathered(g1)), GROUP, scatter_dimension=1, tiled=True)
    block = (1.0 - STEP_SIZE) * x0 + x1
    full = lax.all_gather(block, GROUP, axis=1, tiled=True)
    return (fields + full[None], block)


def solution(mesh):
    placed = (
        P(GROUP, "tile", None),
        P("tile", None),
        P("tile", None),
        P("tile", GROUP, None),
        P("tile", GROUP, None),
        P("tile", GROUP, None),
        P(),
        P(),
    )
    return jax.shard_map(
        on_device,
        mesh=mesh,
        in_specs=placed,
        out_specs=(P(GROUP, "tile", None), P("tile", GROUP)),
        check_vma=False,
    )
```

profile of v0, /device:TPU:1, one launch (start us, length us, event | category | flops | bytes accessed | tf_op | source)
XLA Modules:
  0.0 334.2 jit_solution(7404053742297085599)
XLA Ops:
  7.2 0.0 copy-start
  7.2 0.0 copy-start.3
  7.2 0.0 copy-start.4
  7.2 0.8 add_select_fusion
  8.0 0.7 mul.748
  8.7 0.7 fusion.218
  9.4 0.4 fusion.212
  9.9 15.2 %all_gather.9 = f32[32,1024]{1,0:T(8,128)S(1)} all-gather(f32[32,128]{1,0:T(8,128)S(1)} %slice_negate_fusion), channel_id=1, replica_groups=mesh['member'=4,'tile'=4,'grp'=2] {'member','grp'}, dimensions={1}, use_global_device_ids=true | all-gather | bytes 147456 | tf_op jit(solution)/shard_map/all_gather | solution.py:99
  25.1 0.7 copy-done.7
  25.8 3.2 collective-permute-start.2
  29.0 1.3 collective-permute-start.3
  30.3 1.2 pad_maximum_fusion.3
  31.5 4.0 %collective-permute-start = (f32[12,7,1024]{2,1,0:T(8,128)S(1)}, f32[12,7,1024]{2,1,0:T(8,128)S(1)}, u32[]{:S(2)}, u32[]{:S(2)}) collective-permute-start(f32[12,7,1024]{2,1,0:T(8,128)S(1)} %get-tuple-element.24), channel_id=1, source_target_pairs={{0,2},{2,4},{4,6},{1,3},{3,5},{5,7},{8,10},{10,12},{12,14},{9,11},... | collective-permute-start | bytes 1032200 | tf_op jit(solution)/shard_map/ppermute | solution.py:17
  35.5 1.3 collective-permute-start.1
  36.8 0.6 reduce_sum.47
  37.4 0.1 broadcast_compare_fusion.1
  37.5 0.1 select_reduce_fusion
  37.6 0.7 broadcast_divide_fusion
  38.3 0.1 pad.58.clone
  38.3 0.7 fusion.228
  39.0 0.7 fusion.227
  39.7 4.1 %collective-permute-done = f32[12,7,1024]{2,1,0:T(8,128)S(1)} collective-permute-done((f32[12,7,1024]{2,1,0:T(8,128)S(1)}, f32[12,7,1024]{2,1,0:T(8,128)S(1)}, u32[]{:S(2)}, u32[]{:S(2)}) %collective-permute-start) | collective-permute-done | bytes 344096 | tf_op jit(solution)/shard_map/ppermute | solution.py:17
  43.8 3.9 %collective-permute-done.1 = f32[12,7,1024]{2,1,0:T(8,128)S(1)} collective-permute-done((f32[12,7,1024]{2,1,0:T(8,128)S(1)}, f32[12,7,1024]{2,1,0:T(8,128)S(1)}, u32[]{:S(2)}, u32[]{:S(2)}) %collective-permute-start.1) | collective-permute-done | bytes 344096 | tf_op jit(solution)/shard_map/ppermute | solution.py:18
  47.7 0.3 pad_maximum_fusion
  48.0 0.4 slice.749
  48.4 0.1 maximum_bitcast_fusion.3
  48.5 1.5 fusion.93
  50.0 0.4 slice.752
  50.4 0.1 maximum_bitcast_fusion.1
  50.6 1.5 fusion.99
  52.1 0.3 slice.755
  52.4 0.1 maximum_bitcast_fusion.5
  52.5 1.1 fusion.223
  53.6 0.6 copy-done.6
  54.3 0.0 copy-start.5
  54.3 0.3 subtract_multiply_fusion
  54.6 0.0 all-reduce.12.cloned.1.call-start
  54.7 0.3 copy-done.5
  54.9 0.4 all-reduce.12.cloned.1.call-update
  55.4 0.2 reduce-scatter.3.cloned.1.call-start
  55.6 0.9 pad_maximum_fusion.10
  56.5 55.5 %all-reduce.12.cloned.1.call-done = f32[40,1024]{1,0:T(8,128)} async-done(((f32[40,1024]{1,0:T(8,128)}), f32[40,1024]{1,0:T(8,128)}) %all-reduce.12.cloned.1.call-update) | async-done | bytes 163856 | tf_op jit(solution)/shard_map/psum | solution.py:67
  112.0 1.0 multiply_bitcast_fusion
  113.1 1.7 maximum_maximum_fusion
  114.7 26.1 %fusion.44 = f32[12,36,1024]{2,1,0:T(8,128)S(1)} fusion(f32[12,40,1024]{2,1,0:T(8,128)S(1)} %get-tuple-element.23, f32[36]{0:T(128)S(1)} %and_convert_fusion, f32[]{:T(128)} %bitcast.44, f32[]{:T(128)} %bitcast.43, f32[]{:T(128)} %bitcast.42, f32[]{:T(128)} %bitcast.41, f32[]{:T(128)} %bitcast.40, f32[]{:T(128)} %bitcast.39, f32[]{:T(128)} %bitcast.38, ...), kind=kLoop, calls=%fused_computation.129 | loop fusion | flops 22118400 | bytes 13566564 | tf_op jit(solution)/shard_map/mul | solution.py:81
  140.9 25.1 %fusion.164 = f32[32,1024]{1,0:T(8,128)S(1)} fusion(f32[12,36,1024]{2,1,0:T(8,128)S(1)} %fusion.44, f32[12,40,1024]{2,1,0:T(8,128)} %get-tuple-element.22, f32[]{:T(128)} %bitcast.44, f32[]{:T(128)} %bitcast.43, f32[]{:T(128)} %bitcast.42, f32[]{:T(128)} %bitcast.41, f32[]{:T(128)} %bitcast.40, f32[]{:T(128)} %bitcast.39, f32[]{:T(128)} %bitcast.38, ...), kind=kLoop, calls=%fused_computation.269 | loop fusion | flops 20021248 | bytes 11534436 | tf_op jit(solution)/shard_map/reduce_sum | solution.py:83
  165.9 0.7 broadcast_multiply_fusion.4
  166.6 0.0 reduce-scatter.3.cloned.1.call-update
  166.6 0.0 reduce-scatter.5.cloned.1.call-start
  166.7 33.3 %reduce-scatter.3.cloned.1.call-done = f32[32,128]{1,0:T(8,128)} async-done(((f32[32,1024]{1,0:T(8,128)}), f32[32,128]{1,0:T(8,128)}) %reduce-scatter.3.cloned.1.call-update) | async-done | bytes 16400 | tf_op jit(solution)/shard_map/reduce_scatter | solution.py:101
  200.0 0.7 fusion.219
  200.7 14.9 %all_gather.10 = f32[32,1024]{1,0:T(8,128)S(1)} all-gather(f32[32,128]{1,0:T(8,128)S(1)} %fusion.219), channel_id=1, replica_groups=mesh['member'=4,'tile'=4,'grp'=2] {'member','grp'}, dimensions={1}, use_global_device_ids=true | all-gather | bytes 147456 | tf_op jit(solution)/shard_map/all_gather | solution.py:99
  215.6 3.1 collective-permute-start.4
  218.7 1.5 collective-permute-start.5
  220.2 3.4 %collective-permute-done.5 = f32[4,1024]{1,0:T(4,128)S(1)} collective-permute-done((f32[4,1024]{1,0:T(4,128)S(1)}, f32[4,1024]{1,0:T(4,128)S(1)}, u32[]{:S(2)}, u32[]{:S(2)}) %collective-permute-start.5) | collective-permute-done | bytes 16416 | tf_op jit(solution)/shard_map/ppermute | solution.py:18
  223.6 1.7 broadcast_multiply_fusion
  225.4 26.2 %fusion.89 = f32[12,36,1024]{2,1,0:T(8,128)S(1)} fusion(f32[12,40,1024]{2,1,0:T(8,128)S(1)} %broadcast_multiply_fusion, f32[36]{0:T(128)S(1)} %and_convert_fusion, f32[]{:T(128)} %bitcast.44, f32[]{:T(128)} %bitcast.43, f32[]{:T(128)} %bitcast.42, f32[]{:T(128)} %bitcast.41, f32[]{:T(128)} %bitcast.40, f32[]{:T(128)} %bitcast.39, f32[]{:T(128)} %bitcast.38, ...), kind=kLoop, calls=%fused_computation.174 | loop fusion | flops 22118400 | bytes 13566564 | tf_op jit(solution)/shard_map/mul | solution.py:81
  251.5 25.1 %fusion.210 = f32[32,1024]{1,0:T(8,128)S(1)} fusion(f32[12,36,1024]{2,1,0:T(8,128)S(1)} %fusion.89, f32[12,40,1024]{2,1,0:T(8,128)} %get-tuple-element.22, f32[]{:T(128)} %bitcast.44, f32[]{:T(128)} %bitcast.43, f32[]{:T(128)} %bitcast.42, f32[]{:T(128)} %bitcast.41, f32[]{:T(128)} %bitcast.40, f32[]{:T(128)} %bitcast.39, f32[]{:T(128)} %bitcast.38, ...), kind=kLoop, calls=%fused_computation.315 | loop fusion | flops 20021248 | bytes 11534436 | tf_op jit(solution)/shard_map/reduce_sum | solution.py:83
  276.6 0.7 broadcast_multiply_fusion.3
  277.3 0.0 reduce-scatter.5.cloned.1.call-update
  277.3 32.0 %reduce-scatter.5.cloned.1.call-done = f32[32,128]{1,0:T(8,128)} async-done(((f32[32,1024]{1,0:T(8,128)}), f32[32,128]{1,0:T(8,128)}) %reduce-scatter.5.cloned.1.call-update) | async-done | bytes 16400 | tf_op jit(solution)/shard_map/reduce_scatter | solution.py:103
  309.3 0.7 multiply_add_fusion
  310.0 14.9 %all_gather.11 = f32[32,1024]{1,0:T(8,128)S(1)} all-gather(f32[32,128]{1,0:T(8,128)S(1)} %multiply_add_fusion), channel_id=1, replica_groups=mesh['member'=4,'tile'=4,'grp'=2] {'member','grp'}, dimensions={1}, use_global_device_ids=true | all-gather | bytes 147456 | tf_op jit(solution)/shard_map/all_gather | solution.py:105
  324.9 2.7 slice_add_fusion
  (31 shorter events, 0.2 us)
Async XLA Ops:
  7.2 40.5 %copy-start = (f32[10,32,1024]{2,1,0:T(8,128)S(1)}, f32[10,32,1024]{2,1,0:T(8,128)}, u32[]{:S(2)}) copy-start(f32[10,32,1024]{2,1,0:T(8,128)} %param.8) | copy-start | bytes 3932164
  7.2 40.5 %copy-start.3 = (f32[32,1024]{1,0:T(8,128)S(1)}, f32[32,1024]{1,0:T(8,128)}, u32[]{:S(2)}) copy-start(f32[32,1024]{1,0:T(8,128)} %param.10) | copy-start | bytes 393220
  7.2 40.5 %copy-start.4 = (f32[32,1024]{1,0:T(8,128)S(1)}, f32[32,1024]{1,0:T(8,128)}, u32[]{:S(2)}) copy-start(f32[32,1024]{1,0:T(8,128)} %param.9) | copy-start | bytes 393220
  7.2 29.6 %copy-start.10 = (s32[9,2]{0,1:T(2,128)S(1)}, s32[9,2]{0,1:T(2,128)}, u32[]{:S(2)}) copy-start(s32[9,2]{0,1:T(2,128)} %param.14) | copy-start | bytes 220
  7.2 29.6 %copy-start.11 = (f32[9]{0:T(128)S(1)}, f32[9]{0:T(128)}, u32[]{:S(2)}) copy-start(f32[9]{0:T(128)} %param.15) | copy-start | bytes 112
  25.1 0.7 copy-start.7
  25.8 29.8 %collective-permute-start.2 = (f32[4,1024]{1,0:T(4,128)S(1)}, f32[4,1024]{1,0:T(4,128)S(1)}, u32[]{:S(2)}, u32[]{:S(2)}) collective-permute-start(f32[4,1024]{1,0:T(4,128)S(1)} %get-tuple-element.28), channel_id=1, source_target_pairs={{0,2},{2,4},{4,6},{1,3},{3,5},{5,7},{8,10},{10,12},{12,14},{9,11},... | collective-permute-start | bytes 49160 | tf_op jit(solution)/shard_map/ppermute | solution.py:17
  29.0 26.6 %collective-permute-start.3 = (f32[4,1024]{1,0:T(4,128)S(1)}, f32[4,1024]{1,0:T(4,128)S(1)}, u32[]{:S(2)}, u32[]{:S(2)}) collective-permute-start(f32[4,1024]{1,0:T(4,128)S(1)} %get-tuple-element.29), channel_id=1, source_target_pairs={{2,0},{4,2},{6,4},{3,1},{5,3},{7,5},{10,8},{12,10},{14,12},{11,9},... | collective-permute-start | bytes 49160 | tf_op jit(solution)/shard_map/ppermute | solution.py:18
  31.5 12.3 %collective-permute-start = (f32[12,7,1024]{2,1,0:T(8,128)S(1)}, f32[12,7,1024]{2,1,0:T(8,128)S(1)}, u32[]{:S(2)}, u32[]{:S(2)}) collective-permute-start(f32[12,7,1024]{2,1,0:T(8,128)S(1)} %get-tuple-element.24), channel_id=1, source_target_pairs={{0,2},{2,4},{4,6},{1,3},{3,5},{5,7},{8,10},{10,12},{12,14},{9,11},... | collective-permute-start | bytes 1032200 | tf_op jit(solution)/shard_map/ppermute | solution.py:17
  35.5 12.2 %collective-permute-start.1 = (f32[12,7,1024]{2,1,0:T(8,128)S(1)}, f32[12,7,1024]{2,1,0:T(8,128)S(1)}, u32[]{:S(2)}, u32[]{:S(2)}) collective-permute-start(f32[12,7,1024]{2,1,0:T(8,128)S(1)} %get-tuple-element.25), channel_id=1, source_target_pairs={{2,0},{4,2},{6,4},{3,1},{5,3},{7,5},{10,8},{12,10},{14,12},{11,9},... | collective-permute-start | bytes 1032200 | tf_op jit(solution)/shard_map/ppermute | solution.py:18
  53.6 0.7 copy-start.6
  53.6 1.7 copy-start.2
  54.3 0.7 copy-start.5
  54.6 60.1 %copy-start.1 = (f32[10,40,1024]{2,1,0:T(8,128)}, f32[10,40,1024]{2,1,0:T(8,128)S(1)}, u32[]{:S(2)}) copy-start(f32[10,40,1024]{2,1,0:T(8,128)S(1)} %subtract_multiply_fusion) | copy-start | bytes 4915204
  54.6 57.4 %all-reduce.12.cloned.1.call-start = ((), (), s32[]{:S(2)}) async-start(), calls=%async_computation.2 | async-start | bytes 327680 | tf_op jit(solution)/shard_map/psum | solution.py:67
  55.4 144.6 %reduce-scatter.3.cloned.1.call-start = ((), (), s32[]{:S(2)}) async-start(), calls=%async_computation.3 | async-start | bytes 147456 | tf_op jit(solution)/shard_map/reduce_scatter | solution.py:101
  166.6 142.6 %reduce-scatter.5.cloned.1.call-start = ((), (), s32[]{:S(2)}) async-start(), calls=%async_computation.4 | async-start | bytes 147456 | tf_op jit(solution)/shard_map/reduce_scatter | solution.py:103
  215.6 4.6 %collective-permute-start.4 = (f32[4,1024]{1,0:T(4,128)S(1)}, f32[4,1024]{1,0:T(4,128)S(1)}, u32[]{:S(2)}, u32[]{:S(2)}) collective-permute-start(f32[4,1024]{1,0:T(4,128)S(1)} %get-tuple-element.26), channel_id=1, source_target_pairs={{0,2},{2,4},{4,6},{1,3},{3,5},{5,7},{8,10},{10,12},{12,14},{9,11},... | collective-permute-start | bytes 49160 | tf_op jit(solution)/shard_map/ppermute | solution.py:17
  218.7 4.9 %collective-permute-start.5 = (f32[4,1024]{1,0:T(4,128)S(1)}, f32[4,1024]{1,0:T(4,128)S(1)}, u32[]{:S(2)}, u32[]{:S(2)}) collective-permute-start(f32[4,1024]{1,0:T(4,128)S(1)} %get-tuple-element.27), channel_id=1, source_target_pairs={{2,0},{4,2},{6,4},{3,1},{5,3},{7,5},{10,8},{12,10},{14,12},{11,9},... | collective-permute-start | bytes 49160 | tf_op jit(solution)/shard_map/ppermute | solution.py:18
  251.5 57.7 %copy-start.9 = (f32[32,128]{1,0:T(8,128)S(1)}, f32[32,128]{1,0:T(8,128)}, u32[]{:S(2)}) copy-start(f32[32,128]{1,0:T(8,128)} %reduce-scatter.3.cloned.1.call-done) | copy-start | bytes 49156
  310.0 17.6 %copy-start.8 = (f32[32,128]{1,0:T(8,128)}, f32[32,128]{1,0:T(8,128)S(1)}, u32[]{:S(2)}) copy-start(f32[32,128]{1,0:T(8,128)S(1)} %multiply_add_fusion) | copy-start | bytes 49156
Sparse Core Ops, SparseCore 0:
  59.1 52.8 all-reduce.11
  166.7 33.1 reduce-scatter.2
  277.4 31.8 reduce-scatter.4
where the time goes:
time: 336 us; the launch traced here: 334 us
  waiting for transfers between devices  132 us (39%)
  other arithmetic  123 us (37%)
  blocking collectives  45 us (13%)
  starting transfers between devices  14.7 us (4%)
  between operations  14.1 us (4%)
  local copies, waits for them, and re-layouts  4.14 us (1%)
    psum x1, waiting for transfers between devices, on_device(): mean = lax.psum(own, GROUP) / groups  55.5 us
    mul x3, other arithmetic, apply(): z = spread_out(dev * h[None], taps, -1) * inside  54 us
    reduce_sum x2, other arithmetic, apply(): return jnp.sum(dev[:, reach:reach + rows] * y, axis=0) * -STEP_SIZE  50.1 us
    reduce_scatter x1, waiting for transfers between devices, on_device(): lax.psum_scatter(apply(gathered(-dense_wi)), GROUP, scatter_dimension=1,...  33.3 us
    reduce_scatter x1, waiting for transfers between devices, on_device(): lax.psum_scatter(apply(gathered(g1)), GROUP, scatter_dimension=1, tiled=T...  32 us
    all_gather x2, blocking collectives, gathered(): lax.all_gather(block, GROUP, axis=1, tiled=True)  30.1 us
    all_gather x1, blocking collectives, on_device(): full = lax.all_gather(block, GROUP, axis=1, tiled=True)  14.9 us
    ppermute x3, starting transfers between devices, halo(): above = lax.ppermute(tail, axis, [(i, i + 1) for i in range(count - 1)])  10.3 us
  transfers between devices with their start and end apart: 9, of which 6 were waited for; matrix products, arithmetic and copies ran while one was open for 3% of the time, Pallas kernels for 0%

commit v1 on v0

--- a/solution.py
+++ b/solution.py
@@ -64,7 +64,7 @@
         q = upwind(q, cx[lo:hi], cy[lo:hi])
     fields = q[:, reach : reach + rows]
     own = jnp.sum(q, axis=0) / n
-    mean = lax.psum(own, GROUP) / groups
+    mean = jnp.sum(lax.all_gather(own, GROUP), axis=0) / groups
     dev = (q - own[None]) / math.sqrt(total - 1)
     shift = (own - mean) * math.sqrt(n / (total - 1))
     ones = jnp.full_like(own, 1.0 / math.sqrt(groups))

time: 336 us -> 281 us (0.84)
  waiting for transfers between devices: 132 us -> 78.6 us
    psum x1 -> x0, waiting for transfers between devices: 55.5 us -> none  [on_device(): mean = lax.psum(own, GROUP) / groups]
  transfers between devices with their start and end apart: 9 -> 9, of which waited for: 6 -> 6; matrix products, arithmetic and copies ran while one was open for 3% -> 2% of each run, Pallas kernels for 0% -> 0%
where the time goes in v1:
time: 281 us; the launch traced here: 280 us
  other arithmetic  124 us (44%)
  waiting for transfers between devices  78.6 us (28%)
  blocking collectives  45.4 us (16%)
  starting transfers between devices  14.7 us (5%)
  between operations  14.2 us (5%)
    mul x3, other arithmetic, apply(): z = spread_out(dev * h[None], taps, -1) * inside  53.9 us
    reduce_sum x2, other arithmetic, apply(): return jnp.sum(dev[:, reach:reach + rows] * y, axis=0) * -STEP_SIZE  50 us
    reduce_scatter x1, waiting for transfers between devices, on_device(): lax.psum_scatter(apply(gathered(-dense_wi)), GROUP, scatter_dimension=1,...  32.9 us
    reduce_scatter x1, waiting for transfers between devices, on_device(): lax.psum_scatter(apply(gathered(g1)), GROUP, scatter_dimension=1, tiled=T...  32 us
    all_gather x2, blocking collectives, gathered(): lax.all_gather(block, GROUP, axis=1, tiled=True)  30.5 us
    all_gather x1, blocking collectives, on_device(): full = lax.all_gather(block, GROUP, axis=1, tiled=True)  14.9 us
    ppermute x3, starting transfers between devices, halo(): above = lax.ppermute(tail, axis, [(i, i + 1) for i in range(count - 1)])  10.3 us
    ppermute x3, waiting for transfers between devices, halo(): below = lax.ppermute(head, axis, [(i + 1, i) for i in range(count - 1)])  7.98 us
  transfers between devices with their start and end apart: 9, of which 6 were waited for; matrix products, arithmetic and copies ran while one was open for 2% of the time, Pallas kernels for 0%

profile of v1, /device:TPU:1, one launch (start us, length us, event | category | flops | bytes accessed | tf_op | source)
XLA Modules:
  0.0 280.0 jit_solution(2505273539901154068)
XLA Ops:
  7.2 0.0 all-gather.3.cloned.1.call-start
  7.3 1.3 pad_maximum_fusion.3
  8.6 4.0 %collective-permute-start = (f32[12,7,1024]{2,1,0:T(8,128)S(1)}, f32[12,7,1024]{2,1,0:T(8,128)S(1)}, u32[]{:S(2)}, u32[]{:S(2)}) collective-permute-start(f32[12,7,1024]{2,1,0:T(8,128)S(1)} %get-tuple-element.24), channel_id=1, source_target_pairs={{0,2},{2,4},{4,6},{1,3},{3,5},{5,7},{8,10},{10,12},{12,14},{9,11},... | collective-permute-start | bytes 1032200 | tf_op jit(solution)/shard_map/ppermute | solution.py:17
  12.6 1.3 collective-permute-start.1
  14.0 0.7 fusion.218
  14.7 5.7 %collective-permute-done = f32[12,7,1024]{2,1,0:T(8,128)S(1)} collective-permute-done((f32[12,7,1024]{2,1,0:T(8,128)S(1)}, f32[12,7,1024]{2,1,0:T(8,128)S(1)}, u32[]{:S(2)}, u32[]{:S(2)}) %collective-permute-start) | collective-permute-done | bytes 344096 | tf_op jit(solution)/shard_map/ppermute | solution.py:17
  20.4 3.9 %collective-permute-done.1 = f32[12,7,1024]{2,1,0:T(8,128)S(1)} collective-permute-done((f32[12,7,1024]{2,1,0:T(8,128)S(1)}, f32[12,7,1024]{2,1,0:T(8,128)S(1)}, u32[]{:S(2)}, u32[]{:S(2)}) %collective-permute-start.1) | collective-permute-done | bytes 344096 | tf_op jit(solution)/shard_map/ppermute | solution.py:18
  24.3 0.0 copy-done
  24.3 0.4 pad_maximum_fusion
  24.7 0.4 slice.749
  25.0 0.1 maximum_bitcast_fusion.3
  25.2 1.5 fusion.93
  26.7 0.4 slice.752
  27.1 0.1 maximum_bitcast_fusion.1
  27.2 1.5 fusion.99
  28.7 0.3 slice.755
  29.0 0.1 maximum_bitcast_fusion.5
  29.1 0.0 copy-start.14
  29.1 0.0 copy-start.13
  29.2 1.1 fusion.223
  30.3 0.7 broadcast_multiply_fusion.2
  31.0 0.0 all-gather.3.cloned.1.call-update
  31.0 0.0 reduce-scatter.3.cloned.1.call-start
  31.1 0.4 fusion.212
  31.6 15.7 %all_gather.14 = f32[32,1024]{1,0:T(8,128)S(1)} all-gather(f32[32,128]{1,0:T(8,128)S(1)} %slice_negate_fusion), channel_id=1, replica_groups=mesh['member'=4,'tile'=4,'grp'=2] {'member','grp'}, dimensions={1}, use_global_device_ids=true | all-gather | bytes 147456 | tf_op jit(solution)/shard_map/all_gather | solution.py:99
  47.2 3.1 %collective-permute-start.2 = (f32[4,1024]{1,0:T(4,128)S(1)}, f32[4,1024]{1,0:T(4,128)S(1)}, u32[]{:S(2)}, u32[]{:S(2)}) collective-permute-start(f32[4,1024]{1,0:T(4,128)S(1)} %get-tuple-element.28), channel_id=1, source_target_pairs={{0,2},{2,4},{4,6},{1,3},{3,5},{5,7},{8,10},{10,12},{12,14},{9,11},... | collective-permute-start | bytes 49160 | tf_op jit(solution)/shard_map/ppermute | solution.py:17
  50.3 1.5 collective-permute-start.3
  51.8 0.6 reduce_sum.57
  52.5 0.1 broadcast_compare_fusion.1
  52.5 0.1 select_reduce_fusion
  52.6 0.7 broadcast_divide_fusion
  53.3 0.7 fusion.228
  53.9 0.7 fusion.227
  54.7 0.1 pad.58.clone
  54.7 0.0 collective-permute-done.2
  54.7 0.8 collective-permute-done.3
  55.6 0.7 pad_maximum_fusion.10
  56.3 1.2 subtract_multiply_fusion
  57.5 0.0 copy-done.2
  57.5 0.0 copy-start.1
  57.5 0.0 all-gather.3.cloned.1.call-done
  57.5 2.0 reduce_sum.55
  59.6 1.7 maximum_maximum_fusion
  61.2 26.1 %fusion.44 = f32[12,36,1024]{2,1,0:T(8,128)S(1)} fusion(f32[12,40,1024]{2,1,0:T(8,128)S(1)} %get-tuple-element.23, f32[36]{0:T(128)S(1)} %and_convert_fusion, f32[]{:T(128)} %bitcast.45, f32[]{:T(128)} %bitcast.44, f32[]{:T(128)} %bitcast.43, f32[]{:T(128)} %bitcast.42, f32[]{:T(128)} %bitcast.41, f32[]{:T(128)} %bitcast.40, f32[]{:T(128)} %bitcast.39, ...), kind=kLoop, calls=%fused_computation.129 | loop fusion | flops 22118400 | bytes 13566564 | tf_op jit(solution)/shard_map/mul | solution.py:81
  87.3 25.0 %fusion.164 = f32[32,1024]{1,0:T(8,128)S(1)} fusion(f32[12,36,1024]{2,1,0:T(8,128)S(1)} %fusion.44, f32[12,40,1024]{2,1,0:T(8,128)} %get-tuple-element.22, f32[]{:T(128)} %bitcast.45, f32[]{:T(128)} %bitcast.44, f32[]{:T(128)} %bitcast.43, f32[]{:T(128)} %bitcast.42, f32[]{:T(128)} %bitcast.41, f32[]{:T(128)} %bitcast.40, f32[]{:T(128)} %bitcast.39, ...), kind=kLoop, calls=%fused_computation.269 | loop fusion | flops 20021248 | bytes 11534436 | tf_op jit(solution)/shard_map/reduce_sum | solution.py:83
  112.3 0.7 broadcast_multiply_fusion.4
  113.0 0.0 reduce-scatter.3.cloned.1.call-update
  113.0 0.0 reduce-scatter.5.cloned.1.call-start
  113.0 32.9 %reduce-scatter.3.cloned.1.call-done = f32[32,128]{1,0:T(8,128)} async-done(((f32[32,1024]{1,0:T(8,128)}), f32[32,128]{1,0:T(8,128)}) %reduce-scatter.3.cloned.1.call-update) | async-done | bytes 16400 | tf_op jit(solution)/shard_map/reduce_scatter | solution.py:101
  145.9 0.7 fusion.219
  146.6 14.9 %all_gather.15 = f32[32,1024]{1,0:T(8,128)S(1)} all-gather(f32[32,128]{1,0:T(8,128)S(1)} %fusion.219), channel_id=1, replica_groups=mesh['member'=4,'tile'=4,'grp'=2] {'member','grp'}, dimensions={1}, use_global_device_ids=true | all-gather | bytes 147456 | tf_op jit(solution)/shard_map/all_gather | solution.py:99
  161.5 3.1 %collective-permute-start.4 = (f32[4,1024]{1,0:T(4,128)S(1)}, f32[4,1024]{1,0:T(4,128)S(1)}, u32[]{:S(2)}, u32[]{:S(2)}) collective-permute-start(f32[4,1024]{1,0:T(4,128)S(1)} %get-tuple-element.26), channel_id=1, source_target_pairs={{0,2},{2,4},{4,6},{1,3},{3,5},{5,7},{8,10},{10,12},{12,14},{9,11},... | collective-permute-start | bytes 49160 | tf_op jit(solution)/shard_map/ppermute | solution.py:17
  164.7 1.5 collective-permute-start.5
  166.2 0.0 collective-permute-done.4
  166.2 3.3 %collective-permute-done.5 = f32[4,1024]{1,0:T(4,128)S(1)} collective-permute-done((f32[4,1024]{1,0:T(4,128)S(1)}, f32[4,1024]{1,0:T(4,128)S(1)}, u32[]{:S(2)}, u32[]{:S(2)}) %collective-permute-start.5) | collective-permute-done | bytes 16416 | tf_op jit(solution)/shard_map/ppermute | solution.py:18
  169.5 1.7 broadcast_multiply_fusion
  171.3 26.1 %fusion.89 = f32[12,36,1024]{2,1,0:T(8,128)S(1)} fusion(f32[12,40,1024]{2,1,0:T(8,128)S(1)} %broadcast_multiply_fusion, f32[36]{0:T(128)S(1)} %and_convert_fusion, f32[]{:T(128)} %bitcast.45, f32[]{:T(128)} %bitcast.44, f32[]{:T(128)} %bitcast.43, f32[]{:T(128)} %bitcast.42, f32[]{:T(128)} %bitcast.41, f32[]{:T(128)} %bitcast.40, f32[]{:T(128)} %bitcast.39, ...), kind=kLoop, calls=%fused_computation.174 | loop fusion | flops 22118400 | bytes 13566564 | tf_op jit(solution)/shard_map/mul | solution.py:81
  197.4 25.0 %fusion.210 = f32[32,1024]{1,0:T(8,128)S(1)} fusion(f32[12,36,1024]{2,1,0:T(8,128)S(1)} %fusion.89, f32[12,40,1024]{2,1,0:T(8,128)} %get-tuple-element.22, f32[]{:T(128)} %bitcast.45, f32[]{:T(128)} %bitcast.44, f32[]{:T(128)} %bitcast.43, f32[]{:T(128)} %bitcast.42, f32[]{:T(128)} %bitcast.41, f32[]{:T(128)} %bitcast.40, f32[]{:T(128)} %bitcast.39, ...), kind=kLoop, calls=%fused_computation.315 | loop fusion | flops 20021248 | bytes 11534436 | tf_op jit(solution)/shard_map/reduce_sum | solution.py:83
  222.4 0.7 broadcast_multiply_fusion.3
  223.0 0.0 reduce-scatter.5.cloned.1.call-update
  223.1 32.0 %reduce-scatter.5.cloned.1.call-done = f32[32,128]{1,0:T(8,128)} async-done(((f32[32,1024]{1,0:T(8,128)}), f32[32,128]{1,0:T(8,128)}) %reduce-scatter.5.cloned.1.call-update) | async-done | bytes 16400 | tf_op jit(solution)/shard_map/reduce_scatter | solution.py:103
  255.1 0.7 multiply_add_fusion
  255.8 14.9 %all_gather.16 = f32[32,1024]{1,0:T(8,128)S(1)} all-gather(f32[32,128]{1,0:T(8,128)S(1)} %multiply_add_fusion), channel_id=1, replica_groups=mesh['member'=4,'tile'=4,'grp'=2] {'member','grp'}, dimensions={1}, use_global_device_ids=true | all-gather | bytes 147456 | tf_op jit(solution)/shard_map/all_gather | solution.py:105
  270.7 2.7 slice_add_fusion
  (38 shorter events, 0.2 us)
Async XLA Ops:
  7.2 17.1 %copy-start = (f32[10,32,1024]{2,1,0:T(8,128)S(1)}, f32[10,32,1024]{2,1,0:T(8,128)}, u32[]{:S(2)}) copy-start(f32[10,32,1024]{2,1,0:T(8,128)} %param.8) | copy-start | bytes 3932164
  7.2 17.1 %copy-start.3 = (f32[32,1024]{1,0:T(8,128)S(1)}, f32[32,1024]{1,0:T(8,128)}, u32[]{:S(2)}) copy-start(f32[32,1024]{1,0:T(8,128)} %param.10) | copy-start | bytes 393220
  7.2 17.1 %copy-start.4 = (f32[32,1024]{1,0:T(8,128)S(1)}, f32[32,1024]{1,0:T(8,128)}, u32[]{:S(2)}) copy-start(f32[32,1024]{1,0:T(8,128)} %param.9) | copy-start | bytes 393220
  7.2 6.8 %copy-start.10 = (f32[1,1,1024]{2,1,0:T(1,128)S(1)}, f32[1,1,1024]{2,1,0:T(1,128)}, u32[]{:S(2)}) copy-start(f32[1,1,1024]{2,1,0:T(1,128)} %param.13) | copy-start | bytes 12292
  7.2 6.8 %copy-start.11 = (f32[1,1,1024]{2,1,0:T(1,128)S(1)}, f32[1,1,1024]{2,1,0:T(1,128)}, u32[]{:S(2)}) copy-start(f32[1,1,1024]{2,1,0:T(1,128)} %param.12) | copy-start | bytes 12292
  7.2 6.8 %copy-start.12 = (s32[1,1,1024]{2,1,0:T(1,128)S(1)}, s32[1,1,1024]{2,1,0:T(1,128)}, u32[]{:S(2)}) copy-start(s32[1,1,1024]{2,1,0:T(1,128)} %param.11) | copy-start | bytes 12292
  7.2 50.3 %all-gather.3.cloned.1.call-start = ((), (), s32[]{:S(2)}) async-start(), calls=%async_computation.4 | async-start | bytes 1474560 | tf_op jit(solution)/shard_map/all_gather | solution.py:67
  8.6 11.8 %collective-permute-start = (f32[12,7,1024]{2,1,0:T(8,128)S(1)}, f32[12,7,1024]{2,1,0:T(8,128)S(1)}, u32[]{:S(2)}, u32[]{:S(2)}) collective-permute-start(f32[12,7,1024]{2,1,0:T(8,128)S(1)} %get-tuple-element.24), channel_id=1, source_target_pairs={{0,2},{2,4},{4,6},{1,3},{3,5},{5,7},{8,10},{10,12},{12,14},{9,11},... | collective-permute-start | bytes 1032200 | tf_op jit(solution)/shard_map/ppermute | solution.py:17
  12.6 11.6 %collective-permute-start.1 = (f32[12,7,1024]{2,1,0:T(8,128)S(1)}, f32[12,7,1024]{2,1,0:T(8,128)S(1)}, u32[]{:S(2)}, u32[]{:S(2)}) collective-permute-start(f32[12,7,1024]{2,1,0:T(8,128)S(1)} %get-tuple-element.25), channel_id=1, source_target_pairs={{2,0},{4,2},{6,4},{3,1},{5,3},{7,5},{10,8},{12,10},{14,12},{11,9},... | collective-permute-start | bytes 1032200 | tf_op jit(solution)/shard_map/ppermute | solution.py:18
  29.1 2.0 copy-start.6
  29.1 2.0 copy-start.7
  29.1 22.7 %copy-start.14 = (f32[9]{0:T(128)S(1)}, f32[9]{0:T(128)}, u32[]{:S(2)}) copy-start(f32[9]{0:T(128)} %param.15) | copy-start | bytes 112
  29.1 23.3 %copy-start.13 = (s32[9,2]{0,1:T(2,128)S(1)}, s32[9,2]{0,1:T(2,128)}, u32[]{:S(2)}) copy-start(s32[9,2]{0,1:T(2,128)} %param.14) | copy-start | bytes 220
  30.3 27.2 %copy-start.2 = (f32[10,40,1024]{2,1,0:T(8,128)}, f32[10,40,1024]{2,1,0:T(8,128)S(1)}, u32[]{:S(2)}) copy-start(f32[10,40,1024]{2,1,0:T(8,128)S(1)} %get-tuple-element.3) | copy-start | bytes 4915204
  31.0 114.9 %reduce-scatter.3.cloned.1.call-start = ((), (), s32[]{:S(2)}) async-start(), calls=%async_computation.2 | async-start | bytes 147456 | tf_op jit(solution)/shard_map/reduce_scatter | solution.py:101
  47.2 7.5 %collective-permute-start.2 = (f32[4,1024]{1,0:T(4,128)S(1)}, f32[4,1024]{1,0:T(4,128)S(1)}, u32[]{:S(2)}, u32[]{:S(2)}) collective-permute-start(f32[4,1024]{1,0:T(4,128)S(1)} %get-tuple-element.28), channel_id=1, source_target_pairs={{0,2},{2,4},{4,6},{1,3},{3,5},{5,7},{8,10},{10,12},{12,14},{9,11},... | collective-permute-start | bytes 49160 | tf_op jit(solution)/shard_map/ppermute | solution.py:17
  50.3 5.2 %collective-permute-start.3 = (f32[4,1024]{1,0:T(4,128)S(1)}, f32[4,1024]{1,0:T(4,128)S(1)}, u32[]{:S(2)}, u32[]{:S(2)}) collective-permute-start(f32[4,1024]{1,0:T(4,128)S(1)} %get-tuple-element.29), channel_id=1, source_target_pairs={{2,0},{4,2},{6,4},{3,1},{5,3},{7,5},{10,8},{12,10},{14,12},{11,9},... | collective-permute-start | bytes 49160 | tf_op jit(solution)/shard_map/ppermute | solution.py:18
  57.5 3.8 %copy-start.1 = (f32[10,40,1024]{2,1,0:T(8,128)}, f32[10,40,1024]{2,1,0:T(8,128)S(1)}, u32[]{:S(2)}) copy-start(f32[10,40,1024]{2,1,0:T(8,128)S(1)} %subtract_multiply_fusion) | copy-start | bytes 4915204
  57.5 2.0 copy-start.5
  113.0 142.1 %reduce-scatter.5.cloned.1.call-start = ((), (), s32[]{:S(2)}) async-start(), calls=%async_computation.3 | async-start | bytes 147456 | tf_op jit(solution)/shard_map/reduce_scatter | solution.py:103
  161.5 4.7 %collective-permute-start.4 = (f32[4,1024]{1,0:T(4,128)S(1)}, f32[4,1024]{1,0:T(4,128)S(1)}, u32[]{:S(2)}, u32[]{:S(2)}) collective-permute-start(f32[4,1024]{1,0:T(4,128)S(1)} %get-tuple-element.26), channel_id=1, source_target_pairs={{0,2},{2,4},{4,6},{1,3},{3,5},{5,7},{8,10},{10,12},{12,14},{9,11},... | collective-permute-start | bytes 49160 | tf_op jit(solution)/shard_map/ppermute | solution.py:17
  164.7 4.8 %collective-permute-start.5 = (f32[4,1024]{1,0:T(4,128)S(1)}, f32[4,1024]{1,0:T(4,128)S(1)}, u32[]{:S(2)}, u32[]{:S(2)}) collective-permute-start(f32[4,1024]{1,0:T(4,128)S(1)} %get-tuple-element.27), channel_id=1, source_target_pairs={{2,0},{4,2},{6,4},{3,1},{5,3},{7,5},{10,8},{12,10},{14,12},{11,9},... | collective-permute-start | bytes 49160 | tf_op jit(solution)/shard_map/ppermute | solution.py:18
  197.4 57.7 %copy-start.9 = (f32[32,128]{1,0:T(8,128)S(1)}, f32[32,128]{1,0:T(8,128)}, u32[]{:S(2)}) copy-start(f32[32,128]{1,0:T(8,128)} %reduce-scatter.3.cloned.1.call-done) | copy-start | bytes 49156
  255.8 17.6 %copy-start.8 = (f32[32,128]{1,0:T(8,128)}, f32[32,128]{1,0:T(8,128)S(1)}, u32[]{:S(2)}) copy-start(f32[32,128]{1,0:T(8,128)S(1)} %multiply_add_fusion) | copy-start | bytes 49156
Sparse Core Ops, SparseCore 0:
  31.2 26.3 all-gather.2
  113.1 32.7 reduce-scatter.2
  223.2 31.8 reduce-scatter.4
